TPU v7x, 32 devices: a whole 2x2x4 slice. The times are simulated.
32 devices in a mesh: dp: 8 (over y, x, core), tp: 4 (over z).
Axes of the slice: x: 2, y: 2, z: 4, core: 2. Of those that a mesh axis runs over, the one named last changes fastest.
Arguments:
- layer_in: bfloat16 [32768, 768], P(('dp', 'tp')), may hold values from -6 to 6
- out_grad: bfloat16 [32768, 768], P(('dp', 'tp')), may hold values from -6 to 6
- lengths: int32 [8], P('dp'), may hold values from 2049 to 4096, as said below
- w_query: bfloat16 [768, 768], replicated, may hold values from -0.875 to 0.875
- b_query: bfloat16 [768], replicated, may hold values from -6 to 6
- w_key: bfloat16 [768, 768], replicated, may hold values from -0.21875 to 0.21875
- b_key: bfloat16 [768], replicated, may hold values from -3 to 3
- w_value: bfloat16 [768, 768], replicated, may hold values from -0.21875 to 0.21875
- b_value: bfloat16 [768], replicated, may hold values from -3 to 3
- w_out: bfloat16 [768, 768], replicated, may hold values from -0.875 to 0.875
- b_out: bfloat16 [768], replicated, may hold values from -3 to 3
- seq_proj: bfloat16 [256, 4096], replicated, may hold values from -0.09375 to 0.09375
- attn_gain: bfloat16 [768], replicated, may hold values from 0.5 to 1.5
- attn_shift: bfloat16 [768], replicated, may hold values from -3 to 3
- w_up: bfloat16 [768, 3072], P(None, 'tp'), may hold values from -0.21875 to 0.21875
- b_up: bfloat16 [3072], P('tp'), may hold values from -3 to 3
- w_down: bfloat16 [3072, 768], P('tp'), may hold values from -0.109375 to 0.109375
- b_down: bfloat16 [768], replicated, may hold values from -3 to 3
- ffn_gain: bfloat16 [768], replicated, may hold values from 0.5 to 1.5
- ffn_shift: bfloat16 [768], replicated, may hold values from -3 to 3
Outputs:
- layer_out: bfloat16 [32768, 768], P(('dp', 'tp'))
- grad_in: bfloat16 [32768, 768], P(('dp', 'tp'))
- grad_w_query: float32 [768, 768], replicated
- grad_b_query: float32 [768], replicated
- grad_w_key: float32 [768, 768], replicated
- grad_b_key: float32 [768], replicated
- grad_w_value: float32 [768, 768], replicated
- grad_b_value: float32 [768], replicated
- grad_w_out: float32 [768, 768], replicated
- grad_b_out: float32 [768], replicated
- grad_seq_proj: float32 [256, 4096], replicated
- grad_attn_gain: float32 [768], replicated
- grad_attn_shift: float32 [768], replicated
- grad_w_up: float32 [768, 3072], P(None, 'tp')
- grad_b_up: float32 [3072], P('tp')
- grad_w_down: float32 [3072, 768], P('tp')
- grad_b_down: float32 [768], replicated
- grad_ffn_gain: float32 [768], replicated
- grad_ffn_shift: float32 [768], replicated
Inputs may be any that keep to these rules, and one draw needn't show every extreme that they name: `lengths`: rows from a sequence's length on are padding; some sequence has exactly 4096 rows.
All inputs are finite; a program needn't handle non-finite values.
Results may differ from a plain program's by a relative error of at most 0.022.
The roundings to bfloat16 on the way count: a program that leaves them out, or rounds other values in their place, can miss the bound.
Values may be sent and summed in bfloat16 or wider, within the bound.
A program may use at most 192 MiB of HBM per device.

v0:
```python
import jax
import jax.numpy as jnp
from jax import lax
from jax.sharding import PartitionSpec as P

HEADS = 12
HEAD = 64


def layer_norm(hidden, gain, shift):
    center = hidden - jnp.mean(hidden, axis=-1, keepdims=True)
    spread = jnp.mean(center * center, axis=-1, keepdims=True)
    return center * lax.rsqrt(spread + 1e-05) * gain + shift


def matmul(left, right):
    return jnp.dot(left, right, preferred_element_type=jnp.float32)


def contract_rows(left, right):
    return lax.dot_general(
        left, right, (((0,), (0,)), ((), ())), preferred_element_type=jnp.float32
    )


def times_transpose(left, right):
    return lax.dot_general(
        left, right, (((1,), (1,)), ((), ())), preferred_element_type=jnp.float32
    )


def exact_gelu(value):
    return jax.nn.gelu(value, approximate=False)


def on_device(
    layer_in,
    out_grad,
    lengths,
    w_query,
    b_query,
    w_key,
    b_key,
    w_value,
    b_value,
    w_out,
    b_out,
    seq_proj,
    attn_gain,
    attn_shift,
    w_up,
    b_up,
    w_down,
    b_down,
    ffn_gain,
    ffn_shift,
):
    row_count = layer_in.shape[0]
    width = layer_in.shape[1]
    slots = seq_proj.shape[0]
    tp_parts = lax.axis_size("tp")
    tp_index = lax.axis_index("tp")
    total_rows = row_count * tp_parts
    own_first = tp_index * row_count
    own_positions = own_first + jnp.arange(row_count, dtype=jnp.int32)
    own_live = (own_positions < lengths[0]).astype(jnp.float32)
    own_keys = (matmul(layer_in, w_key) + b_key.astype(jnp.float32)).astype(jnp.bfloat16)
    own_values = (matmul(layer_in, w_value) + b_value.astype(jnp.float32)).astype(jnp.bfloat16)
    own_cols = lax.dynamic_slice_in_dim(seq_proj, own_first, row_count, 1)
    own_proj = (own_cols.astype(jnp.float32) * own_live[None, :]).astype(jnp.bfloat16)
    share_keys = matmul(own_proj, own_keys)
    share_values = matmul(own_proj, own_values)
    proj_keys, proj_values = lax.psum((share_keys, share_values), "tp")
    proj_keys = proj_keys.astype(jnp.bfloat16)
    proj_values = proj_values.astype(jnp.bfloat16)
    queries = (matmul(layer_in, w_query) + b_query.astype(jnp.float32)).astype(jnp.bfloat16)
    block_rows = min(512, row_count)
    block_count = row_count // block_rows
    query_blocks = queries.reshape(block_count, block_rows, HEADS, HEAD)
    key_heads = proj_keys.reshape(slots, HEADS, HEAD)
    value_heads = proj_values.reshape(slots, HEADS, HEAD)

    def attend(query_block):
        logits = (
            jnp.einsum("rhd,khd->rhk", query_block, key_heads, preferred_element_type=jnp.float32)
            * 0.125
        )
        summit = jax.scipy.special.logsumexp(logits, axis=-1)
        weights_b = jnp.exp(logits - summit[..., None]).astype(jnp.bfloat16)
        result = jnp.einsum(
            "rhk,khd->rhd", weights_b, value_heads, preferred_element_type=jnp.float32
        )
        return (result.astype(jnp.bfloat16), summit)

    mixed_blocks, summits = lax.map(attend, query_blocks)
    mixed = mixed_blocks.reshape(row_count, width)
    attn = matmul(mixed, w_out) + b_out.astype(jnp.float32)
    res_one = layer_in.astype(jnp.float32) + attn
    normed, norm_one_pull = jax.vjp(
        layer_norm, res_one, attn_gain.astype(jnp.float32), attn_shift.astype(jnp.float32)
    )
    normed_b = normed.astype(jnp.bfloat16)
    ffn_rows = lax.all_gather(normed_b, "tp", axis=0, tiled=True)
    pre_act = matmul(ffn_rows, w_up) + b_up.astype(jnp.float32)
    hidden_act, gelu_pull = jax.vjp(exact_gelu, pre_act)
    hidden_b = hidden_act.astype(jnp.bfloat16)
    branch = lax.psum_scatter(
        matmul(hidden_b, w_down).astype(jnp.bfloat16), "tp", scatter_dimension=0, tiled=True
    ).astype(jnp.float32)
    branch = branch + b_down.astype(jnp.float32)
    res_two = normed + branch
    final, norm_two_pull = jax.vjp(
        layer_norm, res_two, ffn_gain.astype(jnp.float32), ffn_shift.astype(jnp.float32)
    )
    layer_out = final.astype(jnp.bfloat16)
    d_res_two, g_ffn_gain, g_ffn_shift = norm_two_pull(out_grad.astype(jnp.float32))
    d_branch = d_res_two.astype(jnp.bfloat16)
    g_b_down = jnp.sum(d_branch.astype(jnp.float32), axis=0)
    d_rows = lax.all_gather(d_branch, "tp", axis=0, tiled=True)
    g_w_down = contract_rows(hidden_b, d_rows)
    (d_hidden,) = gelu_pull(times_transpose(d_rows, w_down))
    d_pre = d_hidden.astype(jnp.bfloat16)
    g_b_up = jnp.sum(d_pre.astype(jnp.float32), axis=0)
    g_w_up = contract_rows(ffn_rows, d_pre)
    d_normed_ffn = lax.psum_scatter(
        times_transpose(d_pre, w_up).astype(jnp.bfloat16), "tp", scatter_dimension=0, tiled=True
    ).astype(jnp.float32)
    d_normed = d_res_two + d_normed_ffn
    d_res_one, g_attn_gain, g_attn_shift = norm_one_pull(d_normed)
    d_attn = d_res_one.astype(jnp.bfloat16)
    g_b_out = jnp.sum(d_attn.astype(jnp.float32), axis=0)
    g_w_out = contract_rows(mixed, d_attn)
    d_mixed = times_transpose(d_attn, w_out).astype(jnp.bfloat16)
    d_mixed_blocks = d_mixed.reshape(block_count, block_rows, HEADS, HEAD)

    def attend_back(running, element):
        key_total, value_total = running
        query_block, summit, d_block = element
        logits = (
            jnp.einsum("rhd,khd->rhk", query_block, key_heads, preferred_element_type=jnp.float32)
            * 0.125
        )
        probs = jnp.exp(logits - summit[..., None])
        probs_b = probs.astype(jnp.bfloat16)
        d_probs = jnp.einsum(
            "rhd,khd->rhk", d_block, value_heads, preferred_element_type=jnp.float32
        )
        d_logits = (probs * (d_probs - jnp.sum(probs * d_probs, axis=-1, keepdims=True))).astype(
            jnp.bfloat16
        )
        d_query = (
            jnp.einsum("rhk,khd->rhd", d_logits, key_heads, preferred_element_type=jnp.float32)
            * 0.125
        )
        key_total = (
            key_total
            + jnp.einsum("rhk,rhd->khd", d_logits, query_block, preferred_element_type=jnp.float32)
            * 0.125
        )
        value_total = value_total + jnp.einsum(
            "rhk,rhd->khd", probs_b, d_block, preferred_element_type=jnp.float32
        )
        return ((key_total, value_total), d_query.astype(jnp.bfloat16))

    zero_heads = jnp.zeros((slots, HEADS, HEAD), jnp.float32)
    (key_part, value_part), d_query_blocks = lax.scan(
        attend_back, (zero_heads, zero_heads), (query_blocks, summits, d_mixed_blocks)
    )
    d_queries = d_query_blocks.reshape(row_count, width)
    d_proj_keys, d_proj_values = (
        lax.psum(key_part.reshape(slots, width).astype(jnp.bfloat16), "tp").astype(jnp.float32),
        lax.psum(value_part.reshape(slots, width).astype(jnp.bfloat16), "tp").astype(jnp.float32),
    )
    d_proj_keys = d_proj_keys.astype(jnp.bfloat16)
    d_proj_values = d_proj_values.astype(jnp.bfloat16)
    d_keys = contract_rows(own_proj, d_proj_keys).astype(jnp.bfloat16)
    d_values = contract_rows(own_proj, d_proj_values).astype(jnp.bfloat16)
    own_proj_grad = (
        times_transpose(d_proj_keys, own_keys) + times_transpose(d_proj_values, own_values)
    ) * own_live[None, :]
    g_seq_proj = lax.dynamic_update_slice_in_dim(
        jnp.zeros((slots, total_rows), jnp.float32), own_proj_grad, own_first, 1
    )
    g_w_query = contract_rows(layer_in, d_queries)
    g_b_query = jnp.sum(d_queries.astype(jnp.float32), axis=0)
    g_w_key = contract_rows(layer_in, d_keys)
    g_b_key = jnp.sum(d_keys.astype(jnp.float32), axis=0)
    g_w_value = contract_rows(layer_in, d_values)
    g_b_value = jnp.sum(d_values.astype(jnp.float32), axis=0)
    grad_in = (
        d_res_one
        + times_transpose(d_queries, w_query)
        + times_transpose(d_keys, w_key)
        + times_transpose(d_values, w_value)
    ).astype(jnp.bfloat16)
    (
        g_w_query,
        g_w_key,
        g_w_value,
        g_w_out,
        g_seq_proj,
        g_b_query,
        g_b_key,
        g_b_value,
        g_b_out,
        g_attn_gain,
        g_attn_shift,
        g_ffn_gain,
        g_ffn_shift,
        g_b_down,
    ) = lax.psum(
        (
            g_w_query,
            g_w_key,
            g_w_value,
            g_w_out,
            g_seq_proj,
            g_b_query,
            g_b_key,
            g_b_value,
            g_b_out,
            g_attn_gain,
            g_attn_shift,
            g_ffn_gain,
            g_ffn_shift,
            g_b_down,
        ),
        ("dp", "tp"),
    )
    g_w_up, g_b_up, g_w_down = lax.psum((g_w_up, g_b_up, g_w_down), "dp")
    return (
        layer_out,
        grad_in,
        g_w_query,
        g_b_query,
        g_w_key,
        g_b_key,
        g_w_value,
        g_b_value,
        g_w_out,
        g_b_out,
        g_seq_proj,
        g_attn_gain,
        g_attn_shift,
        g_w_up,
        g_b_up,
        g_w_down,
        g_b_down,
        g_ffn_gain,
        g_ffn_shift,
    )


def solution(mesh):
    in_specs = (
        P(("dp", "tp"), None),
        P(("dp", "tp"), None),
        P("dp"),
        P(),
        P(),
        P(),
        P(),
        P(),
        P(),
        P(),
        P(),
        P(),
        P(),
        P(),
        P(None, "tp"),
        P("tp"),
        P("tp", None),
        P(),
        P(),
        P(),
    )
    out_specs = (
        P(("dp", "tp"), None),
        P(("dp", "tp"), None),
        P(),
        P(),
        P(),
        P(),
        P(),
        P(),
        P(),
        P(),
        P(),
        P(),
        P(),
        P(None, "tp"),
        P("tp"),
        P("tp", None),
        P(),
        P(),
        P(),
    )
    return jax.shard_map(
        on_device, mesh=mesh, in_specs=in_specs, out_specs=out_specs, check_vma=False
    )
```

profile of v0, /device:TPU:0, one launch (start us, length us, event | category | flops | bytes accessed | tf_op | source)
XLA Modules:
  0.0 1117.3 jit_solution(10581152237849772163)
XLA Ops:
  8.8 2.6 copy.66
  11.4 2.8 add_convert_fusion.3
  18.0 62.3 %all-reduce.15 = (bf16[256,768]{1,0:T(8,128)(2,1)S(1)}, bf16[256,768]{1,0:T(8,128)(2,1)}) all-reduce(f32[256,768]{1,0:T(8,128)S(1)} %fusion.73, f32[256,768]{1,0:T(8,128)S(1)} %fusion.72), channel_id=1, replica_groups=mesh['dp'=8,'tp'=4] {'tp'}, use_global_device_ids=true, to_apply=%region_0.0 | all-reduce | flops 393216 | bytes 2359296 | tf_op jit(solution)/shard_map/psum | solution.py:73
  81.7 4.3 add_convert_fusion.5
  87.7 2.4 reshape.176
  93.1 9.8 while.27
  95.9 2.1 fusion.171
  100.8 2.1 fusion.171
  102.9 3.9 copy.71
  112.9 113.9 %all-gather.3.cloned.1.call-done = bf16[4096,768]{0,1:T(8,128)(2,1)} async-done(((bf16[1024,768]{0,1:T(8,128)(2,1)}), bf16[4096,768]{0,1:T(8,128)(2,1)}) %all-gather.3.cloned.1.call-update) | async-done | bytes 6291472 | tf_op jit(solution)/shard_map/all_gather | solution.py:103
  226.8 34.7 %multiply_convert_fusion.1 = (bf16[4096,768]{1,0:T(8,128)(2,1)S(1)}, f32[4096,768]{1,0:T(8,128)}, f32[4096,768]{1,0:T(8,128)}) fusion(f32[768]{0:T(1024)S(1)} %convert_element_type.178, bf16[4096,768]{0,1:T(8,128)(2,1)} %all-gather.3.cloned.1.call-done, bf16[768,768]{1,0:T(8,128)(2,1)S(1)} %copy-done), kind=kOutput, calls=%fused_computation.63 | convolution fusion | flops 5039456256 | bytes 38931456 | tf_op jit(solution)/shard_map/dot_general | solution.py:17
  261.5 2.7 copy-done.75
  264.2 7.0 convolution_convert_fusion.1
  273.7 106.7 %reduce-scatter.3.cloned.1.call-done = bf16[1024,768]{0,1:T(8,128)(2,1)} async-done(((bf16[4096,768]{0,1:T(8,128)(2,1)}), bf16[1024,768]{0,1:T(8,128)(2,1)}) %reduce-scatter.3.cloned.1.call-update) | async-done | bytes 1572880 | tf_op jit(solution)/shard_map/reduce_scatter | solution.py:107
  380.3 3.2 fusion.84
  385.8 2.6 fusion.83
  390.0 2.0 convert_reduce_fusion.2
  392.1 116.0 %all-gather.5.cloned.1.call-done = bf16[4096,768]{0,1:T(8,128)(2,1)} async-done(((bf16[1024,768]{0,1:T(8,128)(2,1)}), bf16[4096,768]{0,1:T(8,128)(2,1)}) %all-gather.5.cloned.1.call-update) | async-done | bytes 6291472 | tf_op jit(solution)/shard_map/all_gather | solution.py:119
  508.1 18.6 %convert_reduce_fusion = (f32[768]{0:T(1024)}, bf16[4096,768]{1,0:T(8,128)(2,1)}) fusion(f32[4096,768]{1,0:T(8,128)} %get-tuple-element.273, f32[4096,768]{1,0:T(8,128)} %get-tuple-element.281, f32[768]{0:T(1024)S(1)} %convert_element_type.178, bf16[4096,768]{0,1:T(8,128)(2,1)} %all-gather.5.cloned.1.call-done, bf16[768,768]{1,0:T(8,128)(2,1)S(1)} %copy-done.66), kind=kOutput, calls=%fused_computation.61 | convolution fusion | flops 4885314560 | bytes 38934528 | tf_op jit(solution)/shard_map/dot_general | solution.py:27
  526.7 9.8 convolution_convert_fusion
  536.7 108.8 %reduce-scatter.5.cloned.1.call-done = bf16[1024,768]{0,1:T(8,128)(2,1)} async-done(((bf16[4096,768]{0,1:T(8,128)(2,1)}), bf16[1024,768]{0,1:T(8,128)(2,1)}) %reduce-scatter.5.cloned.1.call-update) | async-done | bytes 1572880 | tf_op jit(solution)/shard_map/reduce_scatter | solution.py:125
  645.5 5.4 multiply_reduce_fusion
  655.4 2.6 convolution_convert_fusion.4
  659.7 2.4 reshape.180
  662.1 3.0 copy.77
  666.5 33.9 %while.28 = (s32[]{:T(128)}, f32[256,12,64]{0,2,1:T(8,128)}, f32[256,12,64]{0,2,1:T(8,128)S(1)}, bf16[2,512,12,64]{1,3,2,0:T(8,128)(2,1)}, bf16[2,512,12,64]{1,3...) while((s32[]{:T(128)}, f32[256,12,64]{0,2,1:T(8,128)}, ...), condition=%wide.region_18.19_spmd.clone, body=%wide.region_16.18_spmd.clone.sunk | while | flops 1027270656 | bytes 112255784 | solution.py:166
  675.3 4.0 fusion.185
  679.3 4.1 fusion.186
  692.2 4.1 fusion.185
  696.3 4.1 fusion.186
  705.5 2.8 fusion.89
  708.4 2.8 convolution_bitcast_fusion.2
  711.2 36.7 %all-reduce.14.cloned.1.call-done = (bf16[256,768]{0,1:T(8,128)(2,1)}, bf16[256,768]{0,1:T(8,128)(2,1)}) async-done(((bf16[256,768]{0,1:T(8,128)(2,1)}, bf16[256,768]{0,1:T(8,128)(2,1)}), (bf16[256,768]{0,1:T(8,128)(2,1)}, bf16[256,768]{0,1:T(8,128)(2,1)})) %all-reduce.14.cloned.1.call-update) | async-done | bytes 786448 | tf_op jit(solution)/shard_map/psum | solution.py:172
  749.8 2.0 fusion.90
  753.6 2.9 convolution_bitcast_fusion.1
  756.5 2.9 convolution_bitcast_fusion
  759.3 2.5 broadcast_in_dim.31
  763.8 10.1 fusion.92
  773.9 10.2 fusion.91
  784.2 2.7 copy.82
  786.9 14.2 %psum.163 = f32[768]{0:T(1024)} all-reduce(f32[768]{0:T(1024)S(1)} %copy-done.55), channel_id=1, replica_groups=mesh['dp'=8,'tp'=4] {'dp'}, use_global_device_ids=true, to_apply=%region_40.41 | all-reduce | flops 768 | bytes 6144 | tf_op jit(solution)/shard_map/psum | solution.py:230
  801.4 3.1 fusion.87
  810.8 40.6 %all-reduce = (f32[768]{0:T(1024)}, f32[768]{0:T(1024)}, f32[768]{0:T(1024)}, f32[768]{0:T(1024)}, f32[768]{0:T(1024)}, /*index=5*/f32[768]{0:T(1024)}, f32[768]{0:T(1024)}, f32[768]{0:T(1024)}, f32[768]{0:T(1024)}) all-reduce(f32[768]{0:T(1024)S(1)} %reduce_sum.197, ...), channel_id=1, replica_groups=mesh['dp'=8,'tp'=4] {'dp','tp'}, use_global_device_ids=true, to_apply=%region_23.24 | all-reduce | flops 6912 | bytes 55296 | tf_op jit(solution)/shard_map/psum | solution.py:211
  851.4 157.9 %all-reduce.10.cloned.1.call-done = (f32[768,768]{0,1:T(8,128)}, f32[768,768]{0,1:T(8,128)}, f32[768,768]{0,1:T(8,128)}, f32[768,768]{1,0:T(8,128)}, f32[256,4096]{1,0:T(8,128)}) async-done(((f32[768,768]{0,1:T(8,128)}, f32[768,768]{0,1:T(8,128)}, f32[768,768]{0,1:T(8,128)}, f32[768,768]{1,0:T(8,128)}, f32[256,4096]{1,0:T(8,128)}), (f32[768,768]{0,1:T(8,128)}, f32[768,768]{0,1:T(8,128)}, ...) | async-done | bytes 13631504 | tf_op jit(solution)/shard_map/psum | solution.py:211
  1009.3 3.2 copy.84
  1014.4 3.2 copy.86
  1017.6 82.2 %all-reduce.12.cloned.1.call-done = (f32[768,768]{1,0:T(8,128)}, f32[768,768]{1,0:T(8,128)}) async-done(((f32[768,768]{1,0:T(8,128)}, f32[768,768]{1,0:T(8,128)}), (f32[768,768]{1,0:T(8,128)}, f32[768,768]{1,0:T(8,128)})) %all-reduce.12.cloned.1.call-update) | async-done | bytes 4718608 | tf_op jit(solution)/shard_map/psum | solution.py:230
  1102.9 2.1 copy.138
  (256 shorter events, 80.5 us)
Async XLA Ops:
  7.2 219.6 %copy-start = (bf16[768,768]{1,0:T(8,128)(2,1)S(1)}, bf16[768,768]{1,0:T(8,128)(2,1)}, u32[]{:S(2)}) copy-start(bf16[768,768]{1,0:T(8,128)(2,1)} %param.38) | copy-start | bytes 3538948
  7.2 4.2 copy-start.32
  7.2 219.6 %all-gather.3.cloned.1.call-start = ((), (), s32[]{:S(2)}) async-start(), calls=%async_computation.2 | async-start | bytes 7864320 | tf_op jit(solution)/shard_map/all_gather | solution.py:103
  8.1 8.2 copy-start.46
  11.4 3.5 copy-start.56
  11.4 3.5 copy-start.69
  17.4 64.2 %copy-start.57 = (bf16[768]{0:T(1024)(128)(2,1)S(1)}, bf16[768]{0:T(1024)(128)(2,1)}, u32[]{:S(2)}) copy-start(bf16[768]{0:T(1024)(128)(2,1)} %param.28) | copy-start | bytes 4612
  102.9 4.4 copy-start.4
  102.9 4.4 copy-start.7
  102.9 4.4 copy-start.15
  102.9 4.4 copy-start.58
  102.9 4.4 copy-start.37
  102.9 4.4 copy-start.67
  112.4 268.0 %reduce-scatter.3.cloned.1.call-start = ((), (), s32[]{:S(2)}) async-start(), calls=%async_computation.3 | async-start | bytes 7864320 | tf_op jit(solution)/shard_map/reduce_scatter | solution.py:107
  112.9 151.3 %copy-start.65 = (bf16[768,768]{1,0:T(8,128)(2,1)S(1)}, bf16[768,768]{1,0:T(8,128)(2,1)}, u32[]{:S(2)}) copy-start(bf16[768,768]{1,0:T(8,128)(2,1)} %param.40) | copy-start | bytes 3538948
  271.3 236.8 %all-gather.5.cloned.1.call-start = ((), (), s32[]{:S(2)}) async-start(), calls=%async_computation.4 | async-start | bytes 7864320 | tf_op jit(solution)/shard_map/all_gather | solution.py:119
  390.0 118.1 %copy-start.66 = (bf16[768,768]{1,0:T(8,128)(2,1)S(1)}, bf16[768,768]{1,0:T(8,128)(2,1)}, u32[]{:S(2)}) copy-start(bf16[768,768]{1,0:T(8,128)(2,1)} %param.40) | copy-start | bytes 3538948
  392.1 253.5 %reduce-scatter.5.cloned.1.call-start = ((), (), s32[]{:S(2)}) async-start(), calls=%async_computation.5 | async-start | bytes 7864320 | tf_op jit(solution)/shard_map/reduce_scatter | solution.py:125
  536.5 211.4 %all-reduce.14.cloned.1.call-start = ((), (), s32[]{:S(2)}) async-start(), calls=%async_computation.8 | async-start | bytes 1572864 | tf_op jit(solution)/shard_map/psum | solution.py:172
  536.7 114.3 %copy-start.49 = (f32[1024]{0:T(1024)S(1)}, f32[1024]{0:T(1024)}, u32[]{:S(2)}) copy-start(f32[1024]{0:T(1024)} %copy-done.48) | copy-start | bytes 12292
  645.5 5.5 copy-start.10
  645.5 5.5 copy-start.14
  645.5 5.6 copy-start.26
  652.2 3.2 copy-start.68
  662.1 4.4 copy-start.5
  662.1 4.4 copy-start.8
  662.1 4.4 copy-start.16
  662.1 4.4 copy-start.44
  672.1 3.2 copy-start.6
  675.3 4.0 copy-start.12
  689.0 3.2 copy-start.6
  692.2 4.2 copy-start.12
  700.4 3.0 copy-start.19
  703.1 306.1 %all-reduce.10.cloned.1.call-start = ((), (), s32[]{:S(2)}) async-start(), calls=%async_computation.6 | async-start | bytes 27262976 | tf_op jit(solution)/shard_map/psum | solution.py:211
  708.4 39.5 %copy-start.47 = (f32[1024]{0:T(1024)S(1)}, f32[1024]{0:T(1024)}, u32[]{:S(2)}) copy-start(f32[1024]{0:T(1024)} %copy-done.46) | copy-start | bytes 12292
  747.9 4.0 copy-start.45
  749.8 6.6 copy-start.72
  749.8 3.7 copy-start.34
  763.5 336.4 %all-reduce.12.cloned.1.call-start = ((), (), s32[]{:S(2)}) async-start(), calls=%async_computation.7 | async-start | bytes 9437184 | tf_op jit(solution)/shard_map/psum | solution.py:230
  784.2 17.3 %copy-start.70 = (bf16[768,768]{1,0:T(8,128)(2,1)S(1)}, bf16[768,768]{1,0:T(8,128)(2,1)}, u32[]{:S(2)}) copy-start(bf16[768,768]{1,0:T(8,128)(2,1)} %param.29) | copy-start | bytes 3538948
  801.4 3.1 copy-start.71
  801.4 3.1 copy-start.74
  804.6 3.1 copy-start.40
  1009.3 3.2 copy-start.29
  1014.4 85.4 %copy-start.28 = (f32[768,768]{1,0:T(8,128)S(1)}, f32[768,768]{1,0:T(8,128)}, u32[]{:S(2)}) copy-start(f32[768,768]{1,0:T(8,128)} %get-tuple-element.448) | copy-start | bytes 7077892
  1099.9 3.0 copy-start.27
  1102.9 3.2 copy-start.31
  1106.1 3.9 copy-start.1
  (42 other events, 78.2 us)
Sparse Core Ops, SparseCore 0:
  112.5 114.2 all-gather.2
  271.4 108.9 reduce-scatter.2
  392.2 115.8 all-gather.4
  536.6 108.9 reduce-scatter.4
  703.3 44.5 all-reduce.13
  763.6 245.6 all-reduce.9
  1013.0 86.8 all-reduce.11
where the time goes:
time: 1120 us
  waiting for transfers between devices  722 us (64%)
  matrix products  160 us (14%)
  blocking collectives  117 us (10%)
  local copies, waits for them, and re-layouts  70.9 us (6%)
  other arithmetic  28.8 us (3%)
  between operations  16.3 us (1%)
    psum x1, waiting for transfers between devices, on_device(): lax.psum((g_w_query, g_w_key, g_w_value, g_w_out, g_seq_proj, g_b_query,...  158 us
    all_gather x1, waiting for transfers between devices, on_device(): d_rows = lax.all_gather(d_branch, 'tp', axis=0, tiled=True)  116 us
    all_gather x1, waiting for transfers between devices, on_device(): ffn_rows = lax.all_gather(normed_b, 'tp', axis=0, tiled=True)  114 us
    reduce_scatter x1, waiting for transfers between devices, on_device(): lax.psum_scatter(times_transpose(d_pre, w_up).astype(jnp.bfloat16), 'tp',...  109 us
    reduce_scatter x1, waiting for transfers between devices, on_device(): lax.psum_scatter(matmul(hidden_b, w_down).astype(jnp.bfloat16), 'tp', sca...  107 us
    psum x1, waiting for transfers between devices, on_device(): g_w_up, g_b_up, g_w_down = lax.psum((g_w_up, g_b_up, g_w_down), 'dp')  82.2 us
    psum x1, blocking collectives, on_device(): proj_keys, proj_values = lax.psum((share_keys, share_values), 'tp')  62.3 us
    dot_general x8, matrix products, matmul(): return jnp.dot(left, right, preferred_element_type=jnp.float32)  53 us
  transfers between devices with their start and end apart: 7, of which 7 were waited for; matrix products, arithmetic and copies ran while one was open for 4% of the time, Pallas kernels for 0%

commit v1 on v0

--- a/solution.py
+++ b/solution.py
@@ -5,6 +5,28 @@
 
 HEADS = 12
 HEAD = 64
+
+
+def laid_out(blocks, dim):
+    blocks = jnp.moveaxis(blocks, 0, dim)
+    lengths = blocks.shape
+    return blocks.reshape(*lengths[:dim], lengths[dim] * lengths[dim + 1], *lengths[dim + 2 :])
+
+
+def doubled(x, axis):
+    peers = lax.axis_size(axis)
+    blocks = x[None]
+    for level in range(peers.bit_length() - 1):
+        bit = 1 << level
+        other = lax.ppermute(blocks, axis, [(i, i ^ bit) for i in range(peers)])
+        both = jnp.stack([blocks, other])
+        upper = lax.axis_index(axis) >> level & 1
+        blocks = jnp.where(upper == 0, both, both[::-1]).reshape(-1, *x.shape)
+    return blocks
+
+
+def doubled_up(value, axis, dim):
+    return laid_out(doubled(value, axis), dim)
 
 
 def layer_norm(hidden, gain, shift):
@@ -100,7 +122,7 @@
         layer_norm, res_one, attn_gain.astype(jnp.float32), attn_shift.astype(jnp.float32)
     )
     normed_b = normed.astype(jnp.bfloat16)
-    ffn_rows = lax.all_gather(normed_b, "tp", axis=0, tiled=True)
+    ffn_rows = doubled_up(normed_b, "tp", 0)
     pre_act = matmul(ffn_rows, w_up) + b_up.astype(jnp.float32)
     hidden_act, gelu_pull = jax.vjp(exact_gelu, pre_act)
     hidden_b = hidden_act.astype(jnp.bfloat16)

time: 1120 us -> 1190 us (1.062)
  waiting for transfers between devices: 722 us -> 775 us
    ppermute x0 -> x2, waiting for transfers between devices: none -> 163 us  [doubled(): other = lax.ppermute(blocks, axis, [(i, i ^ bit) for i in range(peers)])]
    all_gather x1 -> x0, waiting for transfers between devices: 114 us -> none  [on_device(): ffn_rows = lax.all_gather(normed_b, 'tp', axis=0, tiled=True)]
    unnamed x152 -> x142, local copies, waits for them, and re-layouts: 43 us -> 35.6 us
  transfers between devices with their start and end apart: 7 -> 8, of which waited for: 7 -> 8; matrix products, arithmetic and copies ran while one was open for 4% -> 4% of each run, Pallas kernels for 0% -> 0%
where the time goes in v1:
time: 1190 us; the launch traced here: 1180 us
  waiting for transfers between devices  775 us (65%)
  matrix products  167 us (14%)
  blocking collectives  118 us (10%)
  local copies, waits for them, and re-layouts  63.4 us (5%)
  other arithmetic  39.9 us (3%)
  between operations  16.1 us (1%)
    ppermute x2, waiting for transfers between devices, doubled(): other = lax.ppermute(blocks, axis, [(i, i ^ bit) for i in range(peers)])  163 us
    psum x1, waiting for transfers between devices, on_device(): lax.psum((g_w_query, g_w_key, g_w_value, g_w_out, g_seq_proj, g_b_query,...  157 us
    all_gather x1, waiting for transfers between devices, on_device(): d_rows = lax.all_gather(d_branch, 'tp', axis=0, tiled=True)  116 us
    reduce_scatter x1, waiting for transfers between devices, on_device(): lax.psum_scatter(matmul(hidden_b, w_down).astype(jnp.bfloat16), 'tp', sca...  111 us
    reduce_scatter x1, waiting for transfers between devices, on_device(): lax.psum_scatter(times_transpose(d_pre, w_up).astype(jnp.bfloat16), 'tp',...  109 us
    psum x1, waiting for transfers between devices, on_device(): g_w_up, g_b_up, g_w_down = lax.psum((g_w_up, g_b_up, g_w_down), 'dp')  82.1 us
    psum x1, blocking collectives, on_device(): proj_keys, proj_values = lax.psum((share_keys, share_values), 'tp')  62.1 us
    dot_general x8, matrix products, matmul(): return jnp.dot(left, right, preferred_element_type=jnp.float32)  55.8 us
  transfers between devices with their start and end apart: 8, of which 8 were waited for; matrix products, arithmetic and copies ran while one was open for 4% of the time, Pallas kernels for 0%

profile of v1, /device:TPU:0, one launch (start us, length us, event | category | flops | bytes accessed | tf_op | source)
XLA Modules:
  0.0 1183.3 jit_solution(2949259436623054393)
XLA Ops:
  8.7 3.3 add_convert_fusion.3
  15.8 62.1 %all-reduce.15 = (bf16[256,768]{1,0:T(8,128)(2,1)S(1)}, bf16[256,768]{1,0:T(8,128)(2,1)}) all-reduce(f32[256,768]{1,0:T(8,128)S(1)} %fusion.75, f32[256,768]{1,0:T(8,128)S(1)} %fusion.74), channel_id=1, replica_groups=mesh['dp'=8,'tp'=4] {'tp'}, use_global_device_ids=true, to_apply=%region_0.0 | all-reduce | flops 393216 | bytes 2359296 | tf_op jit(solution)/shard_map/psum | solution.py:95
  79.3 4.3 add_convert_fusion.5
  85.3 2.4 reshape.179
  90.7 10.0 while.27
  100.8 3.9 copy.61
  110.2 2.4 fusion.146
  112.7 30.6 %collective-permute-done = bf16[1,1024,768]{2,1,0:T(8,128)(2,1)S(1)} collective-permute-done((bf16[1,1024,768]{2,1,0:T(8,128)(2,1)}, bf16[1,1024,768]{2,1,0:T(8,128)(2,1)S(1)}, u32[]{:S(2)}, u32[]{:S(2)}) %collective-permute-start) | collective-permute-done | bytes 1572896 | tf_op jit(solution)/shard_map/ppermute | solution.py:21
  143.5 3.3 fusion.71
  146.9 2.6 collective-permute-start.1
  149.5 132.9 %collective-permute-done.1 = bf16[2,1024,768]{2,1,0:T(8,128)(2,1)} collective-permute-done((bf16[2,1024,768]{2,1,0:T(8,128)(2,1)}, bf16[2,1024,768]{2,1,0:T(8,128)(2,1)}, u32[]{:S(2)}, u32[]{:S(2)}) %collective-permute-start.1) | collective-permute-done | bytes 3145760 | tf_op jit(solution)/shard_map/ppermute | solution.py:21
  282.5 3.4 pad_maximum_fusion
  287.3 36.5 %multiply_convert_fusion.1 = (bf16[4096,768]{1,0:T(8,128)(2,1)S(1)}, f32[4096,768]{1,0:T(8,128)}, f32[4096,768]{1,0:T(8,128)}) fusion(f32[768]{0:T(1024)S(1)} %convert_element_type.178, bf16[4096,768]{1,0:T(8,128)(2,1)S(1)} %bitcast.230, bf16[768,768]{1,0:T(8,128)(2,1)S(1)} %copy-done), kind=kOutput, calls=%fused_computation.63 | convolution fusion | flops 5039456256 | bytes 38931456 | tf_op jit(solution)/shard_map/dot_general | solution.py:39
  323.9 2.7 copy-done.72
  326.6 7.4 convolution_convert_fusion.1
  334.7 111.0 %reduce-scatter.3.cloned.1.call-done = bf16[1024,768]{1,0:T(8,128)(2,1)} async-done(((bf16[4096,768]{1,0:T(8,128)(2,1)}), bf16[1024,768]{1,0:T(8,128)(2,1)}) %reduce-scatter.3.cloned.1.call-update) | async-done | bytes 1572880 | tf_op jit(solution)/shard_map/reduce_scatter | solution.py:129
  445.8 3.4 fusion.86
  452.3 2.5 fusion.85
  458.6 116.0 %all-gather.2.cloned.1.call-done = bf16[4096,768]{1,0:T(8,128)(2,1)} async-done(((bf16[1024,768]{1,0:T(8,128)(2,1)}), bf16[4096,768]{1,0:T(8,128)(2,1)}) %all-gather.2.cloned.1.call-update) | async-done | bytes 6291472 | tf_op jit(solution)/shard_map/all_gather | solution.py:141
  574.6 17.6 %convert_reduce_fusion = (f32[768]{0:T(1024)S(1)}, bf16[4096,768]{1,0:T(8,128)(2,1)}) fusion(f32[4096,768]{1,0:T(8,128)} %get-tuple-element.273, f32[4096,768]{1,0:T(8,128)} %get-tuple-element.283, f32[768]{0:T(1024)S(1)} %convert_element_type.178, bf16[4096,768]{1,0:T(8,128)(2,1)} %all-gather.2.cloned.1.call-done, bf16[768,768]{1,0:T(8,128)(2,1)S(1)} %copy-done.66), kind=kOutput, calls=%fused_computation.61 | convolution fusion | flops 4885314560 | bytes 38934528 | tf_op jit(solution)/shard_map/dot_general | solution.py:49
  592.2 9.8 convolution_convert_fusion
  602.0 109.1 %reduce-scatter.5.cloned.1.call-done = bf16[1024,768]{1,0:T(8,128)(2,1)} async-done(((bf16[4096,768]{1,0:T(8,128)(2,1)}), bf16[1024,768]{1,0:T(8,128)(2,1)}) %reduce-scatter.5.cloned.1.call-update) | async-done | bytes 1572880 | tf_op jit(solution)/shard_map/reduce_scatter | solution.py:147
  711.1 4.4 multiply_reduce_fusion
  721.7 2.6 convolution_convert_fusion.4
  726.0 2.4 reshape.184
  728.3 3.0 copy.64
  732.7 33.9 %while.28 = (s32[]{:T(128)}, f32[256,12,64]{0,2,1:T(8,128)}, f32[256,12,64]{0,2,1:T(8,128)S(1)}, bf16[2,512,12,64]{1,3,2,0:T(8,128)(2,1)}, bf16[2,512,12,64]{1,3...) while((s32[]{:T(128)}, f32[256,12,64]{0,2,1:T(8,128)}, ...), condition=%wide.region_18.19_spmd.clone, body=%wide.region_16.18_spmd.clone.sunk | while | flops 1027270656 | bytes 112255784 | solution.py:188
  741.5 4.0 fusion.189
  745.5 4.1 fusion.190
  758.4 4.1 fusion.189
  762.5 4.0 fusion.190
  771.9 2.8 fusion.91
  774.7 2.8 convolution_bitcast_fusion.2
  777.5 36.7 %all-reduce.14.cloned.1.call-done = (bf16[256,768]{0,1:T(8,128)(2,1)}, bf16[256,768]{0,1:T(8,128)(2,1)}) async-done(((bf16[256,768]{0,1:T(8,128)(2,1)}, bf16[256,768]{0,1:T(8,128)(2,1)}), (bf16[256,768]{0,1:T(8,128)(2,1)}, bf16[256,768]{0,1:T(8,128)(2,1)})) %all-reduce.14.cloned.1.call-update) | async-done | bytes 786448 | tf_op jit(solution)/shard_map/psum | solution.py:193
  819.9 2.9 convolution_bitcast_fusion
  822.8 2.9 convolution_bitcast_fusion.1
  825.7 2.5 broadcast_in_dim.60
  830.1 10.1 fusion.93
  840.2 10.3 fusion.94
  850.5 14.2 %psum.163 = f32[768]{0:T(1024)} all-reduce(f32[768]{0:T(1024)S(1)} %get-tuple-element.260), channel_id=1, replica_groups=mesh['dp'=8,'tp'=4] {'dp'}, use_global_device_ids=true, to_apply=%region_40.41 | all-reduce | flops 768 | bytes 6144 | tf_op jit(solution)/shard_map/psum | solution.py:252
  865.1 5.0 fusion.89
  870.1 41.7 %all-reduce = (f32[768]{0:T(1024)}, f32[768]{0:T(1024)}, f32[768]{0:T(1024)}, f32[768]{0:T(1024)}, f32[768]{0:T(1024)}, /*index=5*/f32[768]{0:T(1024)}, f32[768]{0:T(1024)}, f32[768]{0:T(1024)}, f32[768]{0:T(1024)}) all-reduce(f32[768]{0:T(1024)S(1)} %reduce_sum.197, ...), channel_id=1, replica_groups=mesh['dp'=8,'tp'=4] {'dp','tp'}, use_global_device_ids=true, to_apply=%region_23.24 | all-reduce | flops 6912 | bytes 55296 | tf_op jit(solution)/shard_map/psum | solution.py:233
  911.9 3.0 fusion.90
  915.9 2.7 add_convert_fusion.1
  918.7 156.8 %all-reduce.10.cloned.1.call-done = (f32[768,768]{0,1:T(8,128)}, f32[768,768]{0,1:T(8,128)}, f32[768,768]{0,1:T(8,128)}, f32[768,768]{1,0:T(8,128)}, f32[256,4096]{1,0:T(8,128)}) async-done(((f32[768,768]{0,1:T(8,128)}, f32[768,768]{0,1:T(8,128)}, f32[768,768]{0,1:T(8,128)}, f32[768,768]{1,0:T(8,128)}, f32[256,4096]{1,0:T(8,128)}), (f32[768,768]{0,1:T(8,128)}, f32[768,768]{0,1:T(8,128)}, ...) | async-done | bytes 13631504 | tf_op jit(solution)/shard_map/psum | solution.py:233
  1075.5 3.2 copy.66
  1080.6 3.2 copy.68
  1083.8 82.1 %all-reduce.12.cloned.1.call-done = (f32[768,768]{1,0:T(8,128)}, f32[768,768]{1,0:T(8,128)}) async-done(((f32[768,768]{1,0:T(8,128)}, f32[768,768]{1,0:T(8,128)}), (f32[768,768]{1,0:T(8,128)}, f32[768,768]{1,0:T(8,128)})) %all-reduce.12.cloned.1.call-update) | async-done | bytes 4718608 | tf_op jit(solution)/shard_map/psum | solution.py:252
  (252 shorter events, 88.0 us)
Async XLA Ops:
  7.2 280.1 %copy-start = (bf16[768,768]{1,0:T(8,128)(2,1)S(1)}, bf16[768,768]{1,0:T(8,128)(2,1)}, u32[]{:S(2)}) copy-start(bf16[768,768]{1,0:T(8,128)(2,1)} %param.38) | copy-start | bytes 3538948
  7.2 438.5 %reduce-scatter.3.cloned.1.call-start = ((), (), s32[]{:S(2)}) async-start(), calls=%async_computation.2 | async-start | bytes 7864320 | tf_op jit(solution)/shard_map/reduce_scatter | solution.py:129
  8.0 6.1 copy-start.46
  8.7 3.3 copy-start.41
  8.7 3.9 copy-start.53
  8.7 3.9 copy-start.62
  8.7 3.9 copy-start.69
  15.2 64.0 %copy-start.54 = (bf16[768]{0:T(1024)(128)(2,1)S(1)}, bf16[768]{0:T(1024)(128)(2,1)}, u32[]{:S(2)}) copy-start(bf16[768]{0:T(1024)(128)(2,1)} %param.28) | copy-start | bytes 4612
  100.7 4.4 copy-start.4
  100.7 4.4 copy-start.9
  100.7 4.4 copy-start.15
  100.7 4.4 copy-start.55
  100.7 4.4 copy-start.63
  100.8 4.4 copy-start.67
  110.2 33.0 %collective-permute-start = (bf16[1,1024,768]{2,1,0:T(8,128)(2,1)}, bf16[1,1024,768]{2,1,0:T(8,128)(2,1)S(1)}, u32[]{:S(2)}, u32[]{:S(2)}) collective-permute-start(bf16[1,1024,768]{2,1,0:T(8,128)(2,1)} %fusion.147), channel_id=1, source_target_pairs={{0,1},{1,0},{2,3},{3,2},{4,5},{5,4},{6,7},{7,6},{8,9},{9,8},{10,11... | collective-permute-start | bytes 4718600 | tf_op jit(solution)/shard_map/ppermute | solution.py:21
  143.5 6.0 copy-start.58
  146.9 135.6 %collective-permute-start.1 = (bf16[2,1024,768]{2,1,0:T(8,128)(2,1)}, bf16[2,1024,768]{2,1,0:T(8,128)(2,1)}, u32[]{:S(2)}, u32[]{:S(2)}) collective-permute-start(bf16[2,1024,768]{2,1,0:T(8,128)(2,1)} %get-tuple-element.280), channel_id=1, source_target_pairs={{0,2},{1,3},{2,0},{3,1},{4,6},{5,7},{6,4},{7,5},{8,10},{9,11},{10,... | collective-permute-start | bytes 9437192 | tf_op jit(solution)/shard_map/ppermute | solution.py:21
  287.3 36.6 %copy-start.20 = (bf16[2,2,1024,768]{3,2,1,0:T(8,128)(2,1)}, bf16[2,2,1024,768]{3,2,1,0:T(8,128)(2,1)S(1)}, u32[]{:S(2)}) copy-start(bf16[2,2,1024,768]{3,2,1,0:T(8,128)(2,1)S(1)} %reverse_select_fusion) | copy-start | bytes 18874372
  287.3 39.3 %copy-start.66 = (bf16[768,768]{1,0:T(8,128)(2,1)S(1)}, bf16[768,768]{1,0:T(8,128)(2,1)}, u32[]{:S(2)}) copy-start(bf16[768,768]{1,0:T(8,128)(2,1)} %param.40) | copy-start | bytes 3538948
  334.0 240.5 %all-gather.2.cloned.1.call-start = ((), (), s32[]{:S(2)}) async-start(), calls=%async_computation.3 | async-start | bytes 7864320 | tf_op jit(solution)/shard_map/all_gather | solution.py:141
  458.6 252.5 %reduce-scatter.5.cloned.1.call-start = ((), (), s32[]{:S(2)}) async-start(), calls=%async_computation.4 | async-start | bytes 7864320 | tf_op jit(solution)/shard_map/reduce_scatter | solution.py:147
  601.9 212.3 %all-reduce.14.cloned.1.call-start = ((), (), s32[]{:S(2)}) async-start(), calls=%async_computation.7 | async-start | bytes 1572864 | tf_op jit(solution)/shard_map/psum | solution.py:193
  602.0 113.5 %copy-start.49 = (f32[1024]{0:T(1024)S(1)}, f32[1024]{0:T(1024)}, u32[]{:S(2)}) copy-start(f32[1024]{0:T(1024)} %copy-done.48) | copy-start | bytes 12292
  711.1 4.5 copy-start.8
  711.1 5.2 copy-start.14
  711.1 5.6 copy-start.25
  728.3 4.4 copy-start.5
  728.3 4.4 copy-start.10
  728.3 4.4 copy-start.16
  728.3 4.4 copy-start.44
  741.5 4.0 copy-start.12
  758.4 4.2 copy-start.12
  769.5 306.0 %all-reduce.10.cloned.1.call-start = ((), (), s32[]{:S(2)}) async-start(), calls=%async_computation.5 | async-start | bytes 27262976 | tf_op jit(solution)/shard_map/psum | solution.py:233
  774.7 39.5 %copy-start.47 = (f32[1024]{0:T(1024)S(1)}, f32[1024]{0:T(1024)}, u32[]{:S(2)}) copy-start(f32[1024]{0:T(1024)} %copy-done.46) | copy-start | bytes 12292
  814.2 4.0 copy-start.45
  816.2 6.6 copy-start.71
  816.2 3.8 copy-start.65
  829.8 336.1 %all-reduce.12.cloned.1.call-start = ((), (), s32[]{:S(2)}) async-start(), calls=%async_computation.6 | async-start | bytes 9437184 | tf_op jit(solution)/shard_map/psum | solution.py:252
  865.1 5.1 copy-start.50
  865.1 5.1 copy-start.51
  865.1 5.1 copy-start.52
  865.1 46.8 %copy-start.70 = (bf16[768,768]{1,0:T(8,128)(2,1)S(1)}, bf16[768,768]{1,0:T(8,128)(2,1)}, u32[]{:S(2)}) copy-start(bf16[768,768]{1,0:T(8,128)(2,1)} %param.29) | copy-start | bytes 3538948
  911.9 3.3 copy-start.28
  911.9 3.7 copy-start.34
  911.9 4.1 copy-start.40
  1075.5 3.2 copy-start.30
  1080.6 85.3 %copy-start.29 = (f32[768,768]{1,0:T(8,128)S(1)}, f32[768,768]{1,0:T(8,128)}, u32[]{:S(2)}) copy-start(f32[768,768]{1,0:T(8,128)} %get-tuple-element.450) | copy-start | bytes 7077892
  1172.1 3.9 copy-start.1
  (40 other events, 77.9 us)
Sparse Core Ops, SparseCore 0:
  334.2 111.5 reduce-scatter.2
  458.7 115.8 all-gather.1
  602.1 108.9 reduce-scatter.4
  769.6 44.5 all-reduce.13
  829.9 245.5 all-reduce.9
  1079.0 86.8 all-reduce.11
